TPU v7x, 32 devices: a whole 2x2x4 slice. The times are simulated.
32 devices in a mesh: ctx: 8 (over z, y), tp: 4 (over x, core).
Axes of the slice: x: 2, y: 2, z: 4, core: 2. Of those that a mesh axis runs over, the one named last changes fastest.
Arguments:
- qkv: bfloat16 [1024, 3, 8192], P(('ctx', 'tp')), may hold values from -6 to 6
- filters: float32 [3, 7, 8192], P(None, None, 'tp'), may hold values from -1.5 to 1.5
- doc_ids: int32 [8], replicated, may hold values from 0 to 1, never falling along the last dimension, each value on 1 to 5 neighbouring positions
- upstream: bfloat16 [1024, 8192], P('ctx', 'tp'), may hold values from -6 to 6
Outputs:
- attended: bfloat16 [1024, 8192], P('ctx', 'tp')
- qkv_grad: bfloat16 [1024, 3, 8192], P(('ctx', 'tp'))
- filter_grad: float32 [3, 7, 8192], P(None, None, 'tp')
Inputs may be any that keep to these rules, and one draw needn't show every extreme that they name: doc_ids never falls along the sequence; every document covers 1 to 5 whole blocks of 128 tokens.
All inputs are finite; a program needn't handle non-finite values.
Results may differ from a plain program's by a relative error of at most 0.014.
The roundings to bfloat16 on the way count: a program that leaves them out, or rounds other values in their place, can miss the bound.
Values may be sent and summed in bfloat16 or wider, within the bound.
No kernel may reach another device: no remote copies, remote signals or barrier semaphores. Data moves between devices by JAX's collectives and lax.ppermute only.
A program may use at most 128 MiB of HBM per device.

v0:
```python
import jax
import jax.numpy as jnp
from jax import lax
from jax.sharding import PartitionSpec as P

HEAD_DIM = 128
KW = 7
BLOCK = 128
STEPS = 4


def from_behind(value, axis, steps):
    count = lax.axis_size(axis)
    first, last = (max(0, -steps), min(count, count - steps))
    return lax.ppermute(value, axis, [(source, source + steps) for source in range(first, last)])


def block_docs(doc_ids, first_block, count):
    start = jnp.maximum(first_block, 0)
    picked = lax.dynamic_slice_in_dim(doc_ids, start, count)
    return jnp.repeat(picked, BLOCK)


def shards(qkv, filters, doc_ids, upstream):
    local = lax.all_to_all(qkv, "tp", split_axis=2, concat_axis=0, tiled=True)
    tokens = local.shape[0]
    width = local.shape[2]
    heads = width // HEAD_DIM
    blocks_here = tokens // BLOCK
    logit_scale = HEAD_DIM ** (-0.5)
    position = lax.axis_index("ctx")
    reach = STEPS + 1
    rim = from_behind(local[tokens - (KW - 1) :], "ctx", 1)
    inputs = jnp.concatenate([rim, local], axis=0).astype(jnp.float32)
    mixed = sum(
        (filters[:, lag, :] * inputs[KW - 1 - lag : KW - 1 - lag + tokens] for lag in range(KW))
    )
    mixed = mixed.astype(jnp.bfloat16)
    queries = mixed[:, 0].reshape(tokens, heads, HEAD_DIM)
    key_value = mixed[:, 1:3]
    tiles = [key_value]
    current = key_value
    for distance in range(1, STEPS + 1):
        current = from_behind(current, "ctx", 1)
        tiles.append(current)
    joined = jnp.concatenate(tiles, axis=0)
    keys = joined[:, 0].reshape(reach * tokens, heads, HEAD_DIM)
    values = joined[:, 1].reshape(reach * tokens, heads, HEAD_DIM)
    rows = jnp.arange(tokens)
    query_token = position * tokens + rows
    query_doc = block_docs(doc_ids, position * blocks_here, blocks_here)
    key_tokens = jnp.concatenate(
        [(position - distance) * tokens + rows for distance in range(reach)]
    )
    key_docs = jnp.concatenate(
        [
            block_docs(doc_ids, (position - distance) * blocks_here, blocks_here)
            for distance in range(reach)
        ]
    )
    allowed = (
        (key_tokens[None, :] >= 0)
        & (key_tokens[None, :] <= query_token[:, None])
        & (key_docs[None, :] == query_doc[:, None])
    )
    raw = (
        jnp.einsum("qhd,khd->hqk", queries, keys, preferred_element_type=jnp.float32) * logit_scale
    )
    masked = jnp.where(allowed[None], raw, -1e30)
    row_max = masked.max(axis=2)
    expo = jnp.where(allowed[None], jnp.exp(masked - row_max[:, :, None]), 0.0)
    row_sum = expo.sum(axis=2)
    weighted_values = jnp.einsum(
        "hqk,khd->qhd", expo.astype(jnp.bfloat16), values, preferred_element_type=jnp.float32
    )
    attended = (weighted_values / row_sum.T[:, :, None]).astype(jnp.bfloat16)
    grad_out = upstream.reshape(tokens, heads, HEAD_DIM)
    delta = jnp.sum(grad_out.astype(jnp.float32) * attended.astype(jnp.float32), axis=-1).T
    prob = expo / row_sum[:, :, None]
    value_part = jnp.einsum(
        "hqk,qhd->khd", prob.astype(jnp.bfloat16), grad_out, preferred_element_type=jnp.float32
    )
    probability_gradient = jnp.einsum(
        "qhd,khd->hqk", grad_out, values, preferred_element_type=jnp.float32
    )
    score_gradient = (prob * (probability_gradient - delta[:, :, None]) * logit_scale).astype(
        jnp.bfloat16
    )
    query_gradient_rows = jnp.einsum(
        "hqk,khd->qhd", score_gradient, keys, preferred_element_type=jnp.float32
    )
    key_part = jnp.einsum(
        "hqk,qhd->khd", score_gradient, queries, preferred_element_type=jnp.float32
    )
    stacked = jnp.stack(
        [key_part.reshape(reach, tokens, width), value_part.reshape(reach, tokens, width)], axis=2
    )
    partials = [stacked[distance] for distance in range(reach)]
    carried = partials[STEPS]
    for distance in range(STEPS - 1, -1, -1):
        carried = from_behind(carried, "ctx", -1)
        carried = carried + partials[distance]
    conv_grad = jnp.concatenate([query_gradient_rows.reshape(tokens, 1, width), carried], axis=1)
    grad_edge = from_behind(conv_grad[: KW - 1], "ctx", -1)
    extended = jnp.concatenate([conv_grad, grad_edge], axis=0)
    input_grad = sum((filters[:, lag, :] * extended[lag : lag + tokens] for lag in range(KW)))
    tap_terms = jnp.stack(
        [
            jnp.sum(inputs[KW - 1 - lag : KW - 1 - lag + tokens] * conv_grad, axis=0)
            for lag in range(KW)
        ],
        axis=1,
    )
    filter_grad = lax.psum(tap_terms, "ctx")
    qkv_grad = lax.all_to_all(
        input_grad.astype(jnp.bfloat16), "tp", split_axis=0, concat_axis=2, tiled=True
    )
    return (attended.reshape(tokens, width), qkv_grad, filter_grad)


def solution(mesh):
    return jax.shard_map(
        shards,
        mesh=mesh,
        in_specs=(P(("ctx", "tp"), None, None), P(None, None, "tp"), P(), P("ctx", "tp")),
        out_specs=(P("ctx", "tp"), P(("ctx", "tp"), None, None), P(None, None, "tp")),
        check_vma=False,
    )
```

profile of v0, /device:TPU:0, one launch (start us, length us, event | category | flops | bytes accessed | tf_op | source)
XLA Modules:
  0.0 541.6 jit_solution(776772498163065581)
XLA Ops:
  7.2 10.7 %copy.57 = bf16[32,3,8192]{0,1,2:T(4,128)(2,1)} copy(bf16[32,3,8192]{2,0,1:T(8,128)(2,1)} %param.4) | data formatting | bytes 3145728 | tf_op args[0]
  17.8 8.4 %reshape.158 = bf16[4,2,98304]{2,1,0:T(2,128)(2,1)} reshape(bf16[8192,3,32]{2,1,0:T(4,128)(2,1)} %bitcast.114) | data formatting | bytes 3145728
  30.7 19.9 %all-to-all-done = bf16[4,2,98304]{2,1,0:T(2,128)(2,1)S(1)} async-done(((bf16[4,2,98304]{2,1,0:T(2,128)(2,1)}), bf16[4,2,98304]{2,1,0:T(2,128)(2,1)S(1)}, u32[]{:S(2)}, u32[]{:S(2)}) %all-to-all-start) | async-done | bytes 1572896 | tf_op jit(solution)/shard_map/all_to_all | solution.py:25
  50.6 7.1 %reshape.159 = bf16[8192,3,32]{2,1,0:T(4,128)(2,1)} reshape(bf16[4,2,98304]{2,1,0:T(2,128)(2,1)S(1)} %all-to-all-done) | data formatting | bytes 3145728
  57.7 10.5 %copy.59 = bf16[4,32,3,2048]{3,1,0,2:T(8,128)(2,1)S(1)} copy(bf16[4,32,3,2048]{1,2,3,0:T(4,128)(2,1)} %bitcast.113) | data formatting | bytes 3145728 | tf_op jit(solution)/shard_map/all_to_all | solution.py:25
  81.5 5.3 collective-permute-start.1
  86.8 20.0 %collective-permute-done.1 = bf16[128,2,2048]{2,0,1:T(8,128)(2,1)} collective-permute-done((bf16[128,2,2048]{2,0,1:T(8,128)(2,1)S(1)}, bf16[128,2,2048]{2,0,1:T(8,128)(2,1)}, u32[]{:S(2)}, u32[]{:S(2)}) %collective-permute-start.1) | collective-permute-done | bytes 1048608 | tf_op jit(solution)/shard_map/ppermute | solution.py:15
  106.8 5.5 %collective-permute-start.2 = (bf16[128,2,2048]{2,0,1:T(8,128)(2,1)}, bf16[128,2,2048]{2,0,1:T(8,128)(2,1)}, u32[]{:S(2)}, u32[]{:S(2)}) collective-permute-start(bf16[128,2,2048]{2,0,1:T(8,128)(2,1)} %collective-permute-done.1), channel_id=1, source_target_pairs={{0,4},{4,8},{8,12},{12,16},{16,20},{20,24},{24,28},{1,5},{5,9},{9,... | collective-permute-start | bytes 3145736 | tf_op jit(solution)/shard_map/ppermute | solution.py:15
  112.8 19.0 %collective-permute-done.2 = bf16[128,2,2048]{2,0,1:T(8,128)(2,1)} collective-permute-done((bf16[128,2,2048]{2,0,1:T(8,128)(2,1)}, bf16[128,2,2048]{2,0,1:T(8,128)(2,1)}, u32[]{:S(2)}, u32[]{:S(2)}) %collective-permute-start.2) | collective-permute-done | bytes 1048608 | tf_op jit(solution)/shard_map/ppermute | solution.py:15
  131.8 6.2 %collective-permute-start.3 = (bf16[128,2,2048]{2,0,1:T(8,128)(2,1)}, bf16[128,2,2048]{2,0,1:T(8,128)(2,1)}, u32[]{:S(2)}, u32[]{:S(2)}) collective-permute-start(bf16[128,2,2048]{2,0,1:T(8,128)(2,1)} %collective-permute-done.2), channel_id=1, source_target_pairs={{0,4},{4,8},{8,12},{12,16},{16,20},{20,24},{24,28},{1,5},{5,9},{9,... | collective-permute-start | bytes 3145736 | tf_op jit(solution)/shard_map/ppermute | solution.py:15
  141.8 14.7 %collective-permute-done.3 = bf16[128,2,2048]{2,0,1:T(8,128)(2,1)} collective-permute-done((bf16[128,2,2048]{2,0,1:T(8,128)(2,1)}, bf16[128,2,2048]{2,0,1:T(8,128)(2,1)}, u32[]{:S(2)}, u32[]{:S(2)}) %collective-permute-start.3) | collective-permute-done | bytes 1048608 | tf_op jit(solution)/shard_map/ppermute | solution.py:15
  156.5 6.3 %collective-permute-start.4 = (bf16[128,2,2048]{2,0,1:T(8,128)(2,1)}, bf16[128,2,2048]{2,0,1:T(8,128)(2,1)}, u32[]{:S(2)}, u32[]{:S(2)}) collective-permute-start(bf16[128,2,2048]{2,0,1:T(8,128)(2,1)} %collective-permute-done.3), channel_id=1, source_target_pairs={{0,4},{4,8},{8,12},{12,16},{16,20},{20,24},{24,28},{1,5},{5,9},{9,... | collective-permute-start | bytes 3145736 | tf_op jit(solution)/shard_map/ppermute | solution.py:15
  182.7 5.7 %fusion.48 = (bf16[640,1,2048]{2,0,1:T(8,128)(2,1)}, bf16[640,1,2048]{2,0,1:T(8,128)(2,1)}) fusion(bf16[640,2,2048]{2,0,1:T(8,128)(2,1)} %constant_dynamic-update-slice_fusion), kind=kLoop, calls=%fused_computation.106 | loop fusion | bytes 10485760 | tf_op jit(solution)/shard_map/slice | solution.py:47
  197.2 6.6 %fusion.52 = (f32[16,128]{1,0:T(8,128)S(1)}, f32[16,128,640]{2,1,0:T(8,128)}) fusion(pred[128,640]{1,0:T(8,128)(4,1)} %and_and_fusion, bf16[128,16,128]{0,2,1:T(8,128)(2,1)} %bitcast.124, bf16[640,16,128]{0,2,1:T(8,128)(2,1)} %bitcast.115), kind=kOutput, calls=%fused_computation.110 | convolution fusion | flops 342098560 | bytes 8478720 | tf_op jit(solution)/shard_map/sub | solution.py:71
  213.3 5.3 copy.72
  218.6 6.8 %stack_reshape.7 = f32[5,128,1,2048]{3,1,0,2:T(8,128)} reshape(f32[640,16,128]{2,1,0:T(8,128)} %copy.72) | data formatting | bytes 10485760 | tf_op jit(solution)/shard_map/stack;reshape | solution.py:95
  230.5 7.4 %reshape.152 = f32[5,128,1,2048]{1,0,3,2:T(8,128)} reshape(f32[640,16,128]{0,2,1:T(8,128)} %convolution_bitcast_fusion) | data formatting | bytes 10485760 | tf_op jit(solution)/shard_map/stack;reshape | solution.py:95
  237.8 7.9 %copy.73 = f32[5,128,1,2048]{3,1,2,0:T(8,128)} copy(f32[5,128,1,2048]{1,0,3,2:T(8,128)} %reshape.152) | data formatting | bytes 10485760 | tf_op jit(solution)/shard_map/stack;reshape | solution.py:95
  249.1 44.7 %collective-permute-done.5 = f32[128,2,2048]{2,0,1:T(8,128)S(1)} collective-permute-done((f32[128,2,2048]{2,0,1:T(8,128)S(1)}, f32[128,2,2048]{2,0,1:T(8,128)S(1)}, u32[]{:S(2)}, u32[]{:S(2)}) %collective-permute-start.5) | collective-permute-done | bytes 2097184 | tf_op jit(solution)/shard_map/ppermute | solution.py:15
  295.7 44.1 %collective-permute-done.6 = f32[128,2,2048]{2,0,1:T(8,128)S(1)} collective-permute-done((f32[128,2,2048]{2,0,1:T(8,128)S(1)}, f32[128,2,2048]{2,0,1:T(8,128)S(1)}, u32[]{:S(2)}, u32[]{:S(2)}) %collective-permute-start.6) | collective-permute-done | bytes 2097184 | tf_op jit(solution)/shard_map/ppermute | solution.py:15
  341.7 42.9 %collective-permute-done.7 = f32[128,2,2048]{2,0,1:T(8,128)S(1)} collective-permute-done((f32[128,2,2048]{2,0,1:T(8,128)S(1)}, f32[128,2,2048]{2,0,1:T(8,128)S(1)}, u32[]{:S(2)}, u32[]{:S(2)}) %collective-permute-start.7) | collective-permute-done | bytes 2097184 | tf_op jit(solution)/shard_map/ppermute | solution.py:15
  392.0 37.3 %collective-permute-done.8 = f32[128,2,2048]{2,0,1:T(8,128)} collective-permute-done((f32[128,2,2048]{2,0,1:T(8,128)}, f32[128,2,2048]{2,0,1:T(8,128)}, u32[]{:S(2)}, u32[]{:S(2)}) %collective-permute-start.8) | collective-permute-done | bytes 2097184 | tf_op jit(solution)/shard_map/ppermute | solution.py:15
  437.5 6.2 %collective-permute-done.9 = f32[6,3,2048]{2,0,1:T(8,128)S(1)} collective-permute-done((f32[6,3,2048]{2,0,1:T(8,128)S(1)}, f32[6,3,2048]{2,0,1:T(8,128)S(1)}, u32[]{:S(2)}, u32[]{:S(2)}) %collective-permute-start.9) | collective-permute-done | bytes 147488 | tf_op jit(solution)/shard_map/ppermute | solution.py:15
  456.3 74.4 %all-reduce.2.cloned.1.call-done = f32[3,7,2048]{2,0,1:T(4,128)} async-done(((f32[3,7,2048]{2,0,1:T(4,128)}), f32[3,7,2048]{2,0,1:T(4,128)}) %all-reduce.2.cloned.1.call-update) | async-done | bytes 172048 | tf_op jit(solution)/shard_map/psum | solution.py:114
  (115 shorter events, 104.4 us)
Async XLA Ops:
  26.2 24.4 %all-to-all-start = ((bf16[4,2,98304]{2,1,0:T(2,128)(2,1)}), bf16[4,2,98304]{2,1,0:T(2,128)(2,1)S(1)}, u32[]{:S(2)}, u32[]{:S(2)}) async-start(bf16[4,2,98304]{2,1,0:T(2,128)(2,1)} %reshape.158), calls=%async_computation | async-start | bytes 3145728 | tf_op jit(solution)/shard_map/all_to_all | solution.py:25
  68.2 6.4 %collective-permute-start = (bf16[6,3,2048]{2,0,1:T(8,128)(2,1)S(1)}, bf16[6,3,2048]{2,0,1:T(8,128)(2,1)S(1)}, u32[]{:S(2)}, u32[]{:S(2)}) collective-permute-start(bf16[6,3,2048]{2,0,1:T(8,128)(2,1)S(1)} %slice.138), channel_id=1, source_target_pairs={{0,4},{4,8},{8,12},{12,16},{16,20},{20,24},{24,28},{1,5},{5,9},{9,... | collective-permute-start | bytes 221192 | tf_op jit(solution)/shard_map/ppermute | solution.py:15
  72.5 6.7 %copy-start.11 = (f32[3,1,2048]{2,0,1:T(4,128)}, f32[3,1,2048]{2,0,1:T(4,128)S(1)}, u32[]{:S(2)}) copy-start(f32[3,1,2048]{2,0,1:T(4,128)S(1)} %copy.107) | copy-start | bytes 73732
  80.4 57.7 %copy-start.17 = (s32[8]{0:T(128)S(1)}, s32[8]{0:T(128)}, u32[]{:S(2)}) copy-start(s32[8]{0:T(128)} %param.6) | copy-start | bytes 100
  81.5 25.4 %collective-permute-start.1 = (bf16[128,2,2048]{2,0,1:T(8,128)(2,1)S(1)}, bf16[128,2,2048]{2,0,1:T(8,128)(2,1)}, u32[]{:S(2)}, u32[]{:S(2)}) collective-permute-start(bf16[128,2,2048]{2,0,1:T(8,128)(2,1)S(1)} %get-tuple-element.24), channel_id=1, source_target_pairs={{0,4},{4,8},{8,12},{12,16},{16,20},{20,24},{24,28},{1,5},{5,9},{9,... | collective-permute-start | bytes 3145736 | tf_op jit(solution)/shard_map/ppermute | solution.py:15
  106.8 24.9 %collective-permute-start.2 = (bf16[128,2,2048]{2,0,1:T(8,128)(2,1)}, bf16[128,2,2048]{2,0,1:T(8,128)(2,1)}, u32[]{:S(2)}, u32[]{:S(2)}) collective-permute-start(bf16[128,2,2048]{2,0,1:T(8,128)(2,1)} %collective-permute-done.1), channel_id=1, source_target_pairs={{0,4},{4,8},{8,12},{12,16},{16,20},{20,24},{24,28},{1,5},{5,9},{9,... | collective-permute-start | bytes 3145736 | tf_op jit(solution)/shard_map/ppermute | solution.py:15
  131.8 24.7 %collective-permute-start.3 = (bf16[128,2,2048]{2,0,1:T(8,128)(2,1)}, bf16[128,2,2048]{2,0,1:T(8,128)(2,1)}, u32[]{:S(2)}, u32[]{:S(2)}) collective-permute-start(bf16[128,2,2048]{2,0,1:T(8,128)(2,1)} %collective-permute-done.2), channel_id=1, source_target_pairs={{0,4},{4,8},{8,12},{12,16},{16,20},{20,24},{24,28},{1,5},{5,9},{9,... | collective-permute-start | bytes 3145736 | tf_op jit(solution)/shard_map/ppermute | solution.py:15
  156.5 23.9 %collective-permute-start.4 = (bf16[128,2,2048]{2,0,1:T(8,128)(2,1)}, bf16[128,2,2048]{2,0,1:T(8,128)(2,1)}, u32[]{:S(2)}, u32[]{:S(2)}) collective-permute-start(bf16[128,2,2048]{2,0,1:T(8,128)(2,1)} %collective-permute-done.3), channel_id=1, source_target_pairs={{0,4},{4,8},{8,12},{12,16},{16,20},{20,24},{24,28},{1,5},{5,9},{9,... | collective-permute-start | bytes 3145736 | tf_op jit(solution)/shard_map/ppermute | solution.py:15
  245.7 48.1 %slice-start = ((s8[5242880]{0:T(1024)(128)(4,1)}), s8[4194304]{0:T(1024)(128)(4,1)S(1)}, s32[]{:S(2)}) async-start(s8[5242880]{0:T(1024)(128)(4,1)} %bitcast.108), calls=%async_computation.3 | async-start | bytes 8388608
  245.7 48.1 %slice-start.1 = ((s8[5242880]{0:T(1024)(128)(4,1)}), s8[1048576]{0:T(1024)(128)(4,1)S(1)}, s32[]{:S(2)}) async-start(s8[5242880]{0:T(1024)(128)(4,1)} %bitcast.108), calls=%async_computation.4 | async-start | bytes 2097152
  245.7 48.1 %copy-start = (f32[5,128,1,2048]{3,1,2,0:T(8,128)S(1)}, f32[5,128,1,2048]{3,1,2,0:T(8,128)}, u32[]{:S(2)}) copy-start(f32[5,128,1,2048]{3,1,2,0:T(8,128)} %copy.73) | copy-start | bytes 15728644
  247.5 46.3 %collective-permute-start.5 = (f32[128,2,2048]{2,0,1:T(8,128)S(1)}, f32[128,2,2048]{2,0,1:T(8,128)S(1)}, u32[]{:S(2)}, u32[]{:S(2)}) collective-permute-start(f32[128,2,2048]{2,0,1:T(8,128)S(1)} %fusion.25), channel_id=1, source_target_pairs={{4,0},{8,4},{12,8},{16,12},{20,16},{24,20},{28,24},{5,1},{9,5},{13... | collective-permute-start | bytes 6291464 | tf_op jit(solution)/shard_map/ppermute | solution.py:15
  294.2 45.6 %collective-permute-start.6 = (f32[128,2,2048]{2,0,1:T(8,128)S(1)}, f32[128,2,2048]{2,0,1:T(8,128)S(1)}, u32[]{:S(2)}, u32[]{:S(2)}) collective-permute-start(f32[128,2,2048]{2,0,1:T(8,128)S(1)} %fusion.28), channel_id=1, source_target_pairs={{4,0},{8,4},{12,8},{16,12},{20,16},{24,20},{28,24},{5,1},{9,5},{13... | collective-permute-start | bytes 6291464 | tf_op jit(solution)/shard_map/ppermute | solution.py:15
  340.1 47.3 %copy-start.2 = (bf16[640,1,2048]{0,2,1:T(8,128)(2,1)S(1)}, bf16[640,1,2048]{0,2,1:T(8,128)(2,1)}, u32[]{:S(2)}) copy-start(bf16[640,1,2048]{0,2,1:T(8,128)(2,1)} %copy.62) | copy-start | bytes 7864324
  340.1 47.3 %copy-start.3 = (bf16[16,128,640]{2,1,0:T(8,128)(2,1)S(1)}, bf16[16,128,640]{2,1,0:T(8,128)(2,1)}, u32[]{:S(2)}) copy-start(bf16[16,128,640]{2,1,0:T(8,128)(2,1)} %fusion.2) | copy-start | bytes 7864324
  340.1 44.4 %collective-permute-start.7 = (f32[128,2,2048]{2,0,1:T(8,128)S(1)}, f32[128,2,2048]{2,0,1:T(8,128)S(1)}, u32[]{:S(2)}, u32[]{:S(2)}) collective-permute-start(f32[128,2,2048]{2,0,1:T(8,128)S(1)} %fusion.31), channel_id=1, source_target_pairs={{4,0},{8,4},{12,8},{16,12},{20,16},{24,20},{28,24},{5,1},{9,5},{13... | collective-permute-start | bytes 6291464 | tf_op jit(solution)/shard_map/ppermute | solution.py:15
  386.1 43.2 %collective-permute-start.8 = (f32[128,2,2048]{2,0,1:T(8,128)}, f32[128,2,2048]{2,0,1:T(8,128)}, u32[]{:S(2)}, u32[]{:S(2)}) collective-permute-start(f32[128,2,2048]{2,0,1:T(8,128)} %fusion.23), channel_id=1, source_target_pairs={{4,0},{8,4},{12,8},{16,12},{20,16},{24,20},{28,24},{5,1},{9,5},{13... | collective-permute-start | bytes 6291464 | tf_op jit(solution)/shard_map/ppermute | solution.py:15
  392.0 39.8 %copy-start.1 = (f32[128,1,2048]{2,0,1:T(8,128)S(1)}, f32[128,1,2048]{2,0,1:T(8,128)}, u32[]{:S(2)}) copy-start(f32[128,1,2048]{2,0,1:T(8,128)} %copy.75) | copy-start | bytes 3145732
  435.5 8.3 %collective-permute-start.9 = (f32[6,3,2048]{2,0,1:T(8,128)S(1)}, f32[6,3,2048]{2,0,1:T(8,128)S(1)}, u32[]{:S(2)}, u32[]{:S(2)}) collective-permute-start(f32[6,3,2048]{2,0,1:T(8,128)S(1)} %fusion.45), channel_id=1, source_target_pairs={{4,0},{8,4},{12,8},{16,12},{20,16},{24,20},{28,24},{5,1},{9,5},{13... | collective-permute-start | bytes 442376 | tf_op jit(solution)/shard_map/ppermute | solution.py:15
  437.5 6.6 %copy-start.12 = (f32[3,1,2048]{2,0,1:T(4,128)S(1)}, f32[3,1,2048]{2,0,1:T(4,128)}, u32[]{:S(2)}) copy-start(f32[3,1,2048]{2,0,1:T(4,128)} %copy-done.11) | copy-start | bytes 73732
  446.8 7.2 %copy-start.15 = (f32[3,2048]{1,0:T(4,128)S(1)}, f32[3,2048]{1,0:T(4,128)}, u32[]{:S(2)}) copy-start(f32[3,2048]{1,0:T(4,128)} %get-tuple-element.16) | copy-start | bytes 73732
  446.8 7.8 %copy-start.14 = (f32[3,2048]{1,0:T(4,128)S(1)}, f32[3,2048]{1,0:T(4,128)}, u32[]{:S(2)}) copy-start(f32[3,2048]{1,0:T(4,128)} %get-tuple-element.15) | copy-start | bytes 73732
  449.5 82.8 %all-to-all-start.1 = ((bf16[128,3,2048]{2,1,0:T(4,128)(2,1)}), bf16[128,3,2048]{2,1,0:T(4,128)(2,1)S(1)}, u32[]{:S(2)}, u32[]{:S(2)}) async-start(bf16[128,3,2048]{2,1,0:T(4,128)(2,1)} %copy.76), calls=%async_computation.1 | async-start | bytes 4194304 | tf_op jit(solution)/shard_map/all_to_all | solution.py:115
  453.3 77.4 %all-reduce.2.cloned.1.call-start = ((), (), s32[]{:S(2)}) async-start(), calls=%async_computation.2 | async-start | bytes 458752 | tf_op jit(solution)/shard_map/psum | solution.py:114
  (9 other events, 36.9 us)
Sparse Core Ops, SparseCore 0:
  458.1 72.5 all-reduce.1
where the time goes:
time: 544 us; the launch traced here: 542 us
  waiting for transfers between devices  328 us (60%)
  local copies, waits for them, and re-layouts  114 us (21%)
  starting transfers between devices  42.9 us (8%)
  matrix products  22.2 us (4%)
  other arithmetic  20.2 us (4%)
  between operations  14.5 us (3%)
    ppermute x10, waiting for transfers between devices, from_behind(): lax.ppermute(value, axis, [(source, source + steps) for source in range(f...  234 us
    psum x1, waiting for transfers between devices, shards(): filter_grad = lax.psum(tap_terms, 'ctx')  74.4 us
    unnamed x63, local copies, waits for them, and re-layouts  44.5 us
    ppermute x10, starting transfers between devices, from_behind(): lax.ppermute(value, axis, [(source, source + steps) for source in range(f...  34.8 us
    another operation x3, local copies, waits for them, and re-layouts, shards(): jnp.stack([key_part.reshape(reach, tokens, width), value_part.reshape(rea...  22 us
    all_to_all x1, waiting for transfers between devices, shards(): local = lax.all_to_all(qkv, 'tp', split_axis=2, concat_axis=0, tiled=True)  19.9 us
  transfers between devices with their start and end apart: 13, of which 12 were waited for; matrix products, arithmetic and copies ran while one was open for 5% of the time, Pallas kernels for 0%

commit v1 on v0

--- a/solution.py
+++ b/solution.py
@@ -1,3 +1,4 @@
+import functools
 import jax
 import jax.numpy as jnp
 from jax import lax
@@ -7,6 +8,25 @@
 KW = 7
 BLOCK = 128
 STEPS = 4
+
+
+def _cover_lanes(sample, on_dim, pos_dim):
+    val, r1 = (lax.axis_size("tp"), lax.axis_index("tp"))
+    w_next = sample.shape[on_dim] // val
+    long_array = list(sample.shape)
+    long_array[on_dim] = w_next
+    kept_arr = long_array[pos_dim]
+    long_array[pos_dim] = kept_arr * val
+    prior = jnp.zeros(long_array, sample.dtype)
+    for at in range(val):
+        arr_next = lax.dynamic_slice_in_dim(sample, (r1 ^ at) * w_next, w_next, axis=on_dim)
+        if at:
+            arr_next = lax.ppermute(arr_next, "tp", [(j, j ^ at) for j in range(val)])
+        prior = lax.dynamic_update_slice_in_dim(prior, arr_next, (r1 ^ at) * kept_arr, axis=pos_dim)
+    return prior
+
+
+register_case = functools.partial(_cover_lanes, on_dim=2, pos_dim=0)
 
 
 def from_behind(value, axis, steps):
@@ -22,7 +42,7 @@
 
 
 def shards(qkv, filters, doc_ids, upstream):
-    local = lax.all_to_all(qkv, "tp", split_axis=2, concat_axis=0, tiled=True)
+    local = register_case(qkv)
     tokens = local.shape[0]
     width = local.shape[2]
     heads = width // HEAD_DIM

time: 544 us -> 572 us (1.051)
  other arithmetic: 20.2 us -> 56.4 us
  local copies, waits for them, and re-layouts: 114 us -> 122 us
  waiting for transfers between devices: 328 us -> 321 us
    dynamic_update_slice x0 -> x4, local copies, waits for them, and re-layouts: none -> 39.4 us  [_cover_lanes(): lax.dynamic_update_slice_in_dim(prior, arr_next, (r1 ^ at) * kept_arr, ax...]
    unnamed x63 -> x83, local copies, waits for them, and re-layouts: 44.5 us -> 19.1 us
    reduce_sum x1, other arithmetic: 3.59 us -> 25 us  [shards(): jnp.sum(inputs[KW - 1 - lag:KW - 1 - lag + tokens] * conv_grad, axis=0)]
    all_to_all x1 -> x0, waiting for transfers between devices: 19.9 us -> none  [shards(): local = lax.all_to_all(qkv, 'tp', split_axis=2, concat_axis=0, tiled=True)]
    ppermute x10, waiting for transfers between devices: 234 us -> 245 us  [from_behind(): lax.ppermute(value, axis, [(source, source + steps) for source in range(f...]
    all_to_all x1 -> x0, local copies, waits for them, and re-layouts: 10.5 us -> none  [shards(): local = lax.all_to_all(qkv, 'tp', split_axis=2, concat_axis=0, tiled=True)]
    convert_element_type x1, other arithmetic: 2.64 us -> 12.4 us  [shards(): input_grad.astype(jnp.bfloat16)]
    convert_element_type x1, other arithmetic: 2.64 us -> 11.8 us  [shards(): mixed = mixed.astype(jnp.bfloat16)]
  transfers between devices with their start and end apart: 13 -> 15, of which waited for: 12 -> 11; matrix products, arithmetic and copies ran while one was open for 5% -> 9% of each run, Pallas kernels for 0% -> 0%
where the time goes in v1:
time: 572 us; the launch traced here: 571 us
  waiting for transfers between devices  321 us (56%)
  local copies, waits for them, and re-layouts  122 us (21%)
  other arithmetic  56.4 us (10%)
  starting transfers between devices  39.9 us (7%)
  matrix products  17.5 us (3%)
  between operations  14.7 us (3%)
    ppermute x10, waiting for transfers between devices, from_behind(): lax.ppermute(value, axis, [(source, source + steps) for source in range(f...  245 us
    psum x1, waiting for transfers between devices, shards(): filter_grad = lax.psum(tap_terms, 'ctx')  75.5 us
    dynamic_update_slice x4, local copies, waits for them, and re-layouts, _cover_lanes(): lax.dynamic_update_slice_in_dim(prior, arr_next, (r1 ^ at) * kept_arr, ax...  39.4 us
    ppermute x10, starting transfers between devices, from_behind(): lax.ppermute(value, axis, [(source, source + steps) for source in range(f...  33 us
    reduce_sum x1, other arithmetic, shards(): jnp.sum(inputs[KW - 1 - lag:KW - 1 - lag + tokens] * conv_grad, axis=0)  25 us
    another operation x4, local copies, waits for them, and re-layouts, shards(): jnp.stack([key_part.reshape(reach, tokens, width), value_part.reshape(rea...  24.6 us
    unnamed x83, local copies, waits for them, and re-layouts  19.1 us
    convert_element_type x1, other arithmetic, shards(): input_grad.astype(jnp.bfloat16)  12.4 us
  transfers between devices with their start and end apart: 15, of which 11 were waited for; matrix products, arithmetic and copies ran while one was open for 9% of the time, Pallas kernels for 0%

profile of v1, /device:TPU:0, one launch (start us, length us, event | category | flops | bytes accessed | tf_op | source)
XLA Modules:
  0.0 570.9 jit_solution(11901681186360844059)
XLA Ops:
  15.1 6.1 %dynamic_update_slice.12 = bf16[128,3,2048]{0,2,1:T(8,128)(2,1)S(1)} dynamic-update-slice(bf16[128,3,2048]{0,2,1:T(8,128)(2,1)S(1)} %broadcast_in_dim.20, bf16[32,3,2048]{0,2,1:T(8,128)(2,1)S(1)} %copy.102, s32[]{:T(128)S(6)} %select_n.38, s32[]{:T(128)} %constant.13.clone.1, s32[]{:T(128)} %constant.13.clone.1) | dynamic-update-slice | bytes 786436 | tf_op jit(solution)/shard_map/dynamic_update_slice | solution.py:25
  24.4 11.1 %dynamic_update_slice.13 = bf16[128,3,2048]{0,2,1:T(8,128)(2,1)S(1)} dynamic-update-slice(bf16[128,3,2048]{0,2,1:T(8,128)(2,1)S(1)} %dynamic_update_slice.12, bf16[32,3,2048]{0,2,1:T(8,128)(2,1)S(1)} %copy.62, s32[]{:T(128)S(6)} %select_n.40, s32[]{:T(128)} %constant.13.clone.1, s32[]{:T(128)} %constant.13.clone.1) | dynamic-update-slice | bytes 786436 | tf_op jit(solution)/shard_map/dynamic_update_slice | solution.py:25
  37.2 11.1 %dynamic_update_slice.14 = bf16[128,3,2048]{0,2,1:T(8,128)(2,1)S(1)} dynamic-update-slice(bf16[128,3,2048]{0,2,1:T(8,128)(2,1)S(1)} %dynamic_update_slice.13, bf16[32,3,2048]{0,2,1:T(8,128)(2,1)S(1)} %copy.63, s32[]{:T(128)S(6)} %select_n.42, s32[]{:T(128)} %constant.13.clone.1, s32[]{:T(128)} %constant.13.clone.1) | dynamic-update-slice | bytes 786436 | tf_op jit(solution)/shard_map/dynamic_update_slice | solution.py:25
  50.0 11.1 %dynamic_update_slice.15 = bf16[128,3,2048]{0,2,1:T(8,128)(2,1)S(1)} dynamic-update-slice(bf16[128,3,2048]{0,2,1:T(8,128)(2,1)S(1)} %dynamic_update_slice.14, bf16[32,3,2048]{0,2,1:T(8,128)(2,1)S(1)} %copy.64, s32[]{:T(128)S(6)} %select_n.44, s32[]{:T(128)} %constant.13.clone.1, s32[]{:T(128)} %constant.13.clone.1) | dynamic-update-slice | bytes 786436 | tf_op jit(solution)/shard_map/dynamic_update_slice | solution.py:25
  70.7 11.8 %add_convert_fusion = bf16[128,3,2048]{0,2,1:T(8,128)(2,1)S(1)} fusion(f32[134,3,2048]{0,2,1:T(8,128)S(1)} %maximum_convert_fusion, f32[3,2048]{1,0:T(4,128)S(1)} %get-tuple-element.48, f32[3,2048]{1,0:T(4,128)S(1)} %get-tuple-element.49, f32[3,2048]{1,0:T(4,128)S(1)} %copy-done.12, f32[3,2048]{1,0:T(4,128)S(1)} %copy-done.13, f32[3,2048]{1,0:T(4,128)S(1)} %copy-done.14, ...), kind=kLoop, calls=%fused_computation.41 | loop fusion | flops 11010048 | bytes 23764992 | tf_op jit(solution)/shard_map/convert_element_type | solution.py:58
  88.3 21.1 %collective-permute-done.4 = bf16[128,2,2048]{0,2,1:T(8,128)(2,1)S(1)} collective-permute-done((bf16[128,2,2048]{0,2,1:T(8,128)(2,1)S(1)}, bf16[128,2,2048]{0,2,1:T(8,128)(2,1)S(1)}, u32[]{:S(2)}, u32[]{:S(2)}) %collective-permute-start.4) | collective-permute-done | bytes 1048608 | tf_op jit(solution)/shard_map/ppermute | solution.py:35
  109.3 5.5 collective-permute-start.5
  114.8 19.1 %collective-permute-done.5 = bf16[128,2,2048]{0,2,1:T(8,128)(2,1)} collective-permute-done((bf16[128,2,2048]{0,2,1:T(8,128)(2,1)S(1)}, bf16[128,2,2048]{0,2,1:T(8,128)(2,1)}, u32[]{:S(2)}, u32[]{:S(2)}) %collective-permute-start.5) | collective-permute-done | bytes 1048608 | tf_op jit(solution)/shard_map/ppermute | solution.py:35
  133.9 6.2 %collective-permute-start.6 = (bf16[128,2,2048]{0,2,1:T(8,128)(2,1)}, bf16[128,2,2048]{0,2,1:T(8,128)(2,1)}, u32[]{:S(2)}, u32[]{:S(2)}) collective-permute-start(bf16[128,2,2048]{0,2,1:T(8,128)(2,1)} %collective-permute-done.5), channel_id=1, source_target_pairs={{0,4},{4,8},{8,12},{12,16},{16,20},{20,24},{24,28},{1,5},{5,9},{9,... | collective-permute-start | bytes 3145736 | tf_op jit(solution)/shard_map/ppermute | solution.py:35
  144.0 14.7 %collective-permute-done.6 = bf16[128,2,2048]{0,2,1:T(8,128)(2,1)} collective-permute-done((bf16[128,2,2048]{0,2,1:T(8,128)(2,1)}, bf16[128,2,2048]{0,2,1:T(8,128)(2,1)}, u32[]{:S(2)}, u32[]{:S(2)}) %collective-permute-start.6) | collective-permute-done | bytes 1048608 | tf_op jit(solution)/shard_map/ppermute | solution.py:35
  158.8 6.3 %collective-permute-start.7 = (bf16[128,2,2048]{0,2,1:T(8,128)(2,1)}, bf16[128,2,2048]{0,2,1:T(8,128)(2,1)}, u32[]{:S(2)}, u32[]{:S(2)}) collective-permute-start(bf16[128,2,2048]{0,2,1:T(8,128)(2,1)} %collective-permute-done.6), channel_id=1, source_target_pairs={{0,4},{4,8},{8,12},{12,16},{16,20},{20,24},{24,28},{1,5},{5,9},{9,... | collective-permute-start | bytes 3145736 | tf_op jit(solution)/shard_map/ppermute | solution.py:35
  172.7 10.1 %collective-permute-done.7 = bf16[128,2,2048]{0,2,1:T(8,128)(2,1)} collective-permute-done((bf16[128,2,2048]{0,2,1:T(8,128)(2,1)}, bf16[128,2,2048]{0,2,1:T(8,128)(2,1)}, u32[]{:S(2)}, u32[]{:S(2)}) %collective-permute-start.7) | collective-permute-done | bytes 1048608 | tf_op jit(solution)/shard_map/ppermute | solution.py:35
  202.9 5.3 copy.76
  208.2 6.8 %stack_reshape.7 = f32[5,128,1,2048]{3,1,0,2:T(8,128)} reshape(f32[640,16,128]{2,1,0:T(8,128)} %copy.76) | data formatting | bytes 10485760 | tf_op jit(solution)/shard_map/stack;reshape | solution.py:115
  214.9 5.9 %copy.78 = f32[5,128,1,2048]{1,3,2,0:T(8,128)} copy(f32[5,128,1,2048]{3,1,0,2:T(8,128)} %stack_reshape.7) | data formatting | bytes 10485760 | tf_op jit(solution)/shard_map/stack;reshape | solution.py:115
  224.0 7.4 %reshape.152 = f32[5,128,1,2048]{1,0,3,2:T(8,128)} reshape(f32[640,16,128]{0,2,1:T(8,128)} %convolution_bitcast_fusion) | data formatting | bytes 10485760 | tf_op jit(solution)/shard_map/stack;reshape | solution.py:115
  237.5 44.7 %collective-permute-done.8 = f32[128,2,2048]{0,2,1:T(8,128)S(1)} collective-permute-done((f32[128,2,2048]{0,2,1:T(8,128)S(1)}, f32[128,2,2048]{0,2,1:T(8,128)S(1)}, u32[]{:S(2)}, u32[]{:S(2)}) %collective-permute-start.8) | collective-permute-done | bytes 2097184 | tf_op jit(solution)/shard_map/ppermute | solution.py:35
  283.6 44.4 %collective-permute-done.9 = f32[128,2,2048]{0,2,1:T(8,128)S(1)} collective-permute-done((f32[128,2,2048]{0,2,1:T(8,128)S(1)}, f32[128,2,2048]{0,2,1:T(8,128)S(1)}, u32[]{:S(2)}, u32[]{:S(2)}) %collective-permute-start.9) | collective-permute-done | bytes 2097184 | tf_op jit(solution)/shard_map/ppermute | solution.py:35
  329.8 44.4 %collective-permute-done.10 = f32[128,2,2048]{0,2,1:T(8,128)S(1)} collective-permute-done((f32[128,2,2048]{0,2,1:T(8,128)S(1)}, f32[128,2,2048]{0,2,1:T(8,128)S(1)}, u32[]{:S(2)}, u32[]{:S(2)}) %collective-permute-start.10) | collective-permute-done | bytes 2097184 | tf_op jit(solution)/shard_map/ppermute | solution.py:35
  377.8 39.7 %collective-permute-done.11 = f32[128,2,2048]{0,2,1:T(8,128)S(1)} collective-permute-done((f32[128,2,2048]{0,2,1:T(8,128)S(1)}, f32[128,2,2048]{0,2,1:T(8,128)S(1)}, u32[]{:S(2)}, u32[]{:S(2)}) %collective-permute-start.11) | collective-permute-done | bytes 2097184 | tf_op jit(solution)/shard_map/ppermute | solution.py:35
  417.9 25.0 %multiply_reduce_fusion = (f32[3,2048]{1,0:T(4,128)}, f32[3,2048]{1,0:T(4,128)}, f32[3,2048]{1,0:T(4,128)}, f32[3,2048]{1,0:T(4,128)}, f32[3,2048]{1,0:T(4,128)}, /*index=5*/f32[3,2048]{1,0:T(4,128)}, f32[3,2048]{1,0:T(4,128)}) fusion(f32[134,3,2048]{0,2,1:T(8,128)} %copy-done, f32[128,2,2048]{0,2,1:T(8,128)S(1)} %fusion.34, f32[128,1,2048]{0,2,1:T(8,128)} %bitcast.100), kind=kLoop, calls=%fused_computation.34 | loop fusion | flops 11753472 | bytes 25337856 | tf_op jit(solution)/shard_map/reduce_sum | solution.py:129
  451.3 5.0 collective-permute-done.12
  461.9 12.4 %fusion.6 = bf16[128,3,2048]{0,2,1:T(8,128)(2,1)} fusion(f32[134,3,2048]{0,2,1:T(8,128)S(1)} %pad_maximum_fusion, f32[3,2048]{1,0:T(4,128)S(1)} %get-tuple-element.48, f32[3,2048]{1,0:T(4,128)S(1)} %copy-done.17, f32[3,2048]{1,0:T(4,128)S(1)} %copy-done.12, f32[3,2048]{1,0:T(4,128)S(1)} %copy-done.13, f32[3,2048]{1,0:T(4,128)S(1)} %copy-done.14, ...), kind=kLoop, calls=%fused_computation.22 | loop fusion | flops 11796480 | bytes 23764992 | tf_op jit(solution)/shard_map/convert_element_type | solution.py:136
  484.5 75.5 %all-reduce.2.cloned.1.call-done = f32[3,7,2048]{2,0,1:T(4,128)} async-done(((f32[3,7,2048]{2,0,1:T(4,128)}), f32[3,7,2048]{2,0,1:T(4,128)}) %all-reduce.2.cloned.1.call-update) | async-done | bytes 172048 | tf_op jit(solution)/shard_map/psum | solution.py:134
  (148 shorter events, 105.4 us)
Async XLA Ops:
  9.6 38.7 %collective-permute-start.2 = (bf16[32,3,2048]{2,0,1:T(8,128)(2,1)S(1)}, bf16[32,3,2048]{2,0,1:T(8,128)(2,1)}, u32[]{:S(2)}, u32[]{:S(2)}) collective-permute-start(bf16[32,3,2048]{2,0,1:T(8,128)(2,1)S(1)} %get-tuple-element.26), channel_id=1, source_target_pairs={{0,3},{1,2},{2,1},{3,0},{4,7},{5,6},{6,5},{7,4},{8,11},{9,10},{10,... | collective-permute-start | bytes 1179656 | tf_op jit(solution)/shard_map/ppermute | solution.py:24
  12.0 10.7 %collective-permute-start = (bf16[32,3,2048]{2,0,1:T(8,128)(2,1)}, bf16[32,3,2048]{2,0,1:T(8,128)(2,1)}, u32[]{:S(2)}, u32[]{:S(2)}) collective-permute-start(bf16[32,3,2048]{2,0,1:T(8,128)(2,1)} %get-tuple-element.27), channel_id=1, source_target_pairs={{0,1},{1,0},{2,3},{3,2},{4,5},{5,4},{6,7},{7,6},{8,9},{9,8},{10,11... | collective-permute-start | bytes 1179656 | tf_op jit(solution)/shard_map/ppermute | solution.py:24
  12.7 22.8 %collective-permute-start.1 = (bf16[32,3,2048]{2,0,1:T(8,128)(2,1)}, bf16[32,3,2048]{2,0,1:T(8,128)(2,1)}, u32[]{:S(2)}, u32[]{:S(2)}) collective-permute-start(bf16[32,3,2048]{2,0,1:T(8,128)(2,1)} %get-tuple-element.29), channel_id=1, source_target_pairs={{0,2},{1,3},{2,0},{3,1},{4,6},{5,7},{6,4},{7,5},{8,10},{9,11},{10,... | collective-permute-start | bytes 1179656 | tf_op jit(solution)/shard_map/ppermute | solution.py:24
  62.4 6.2 %collective-permute-start.3 = (bf16[6,3,2048]{2,0,1:T(8,128)(2,1)S(1)}, bf16[6,3,2048]{2,0,1:T(8,128)(2,1)S(1)}, u32[]{:S(2)}, u32[]{:S(2)}) collective-permute-start(bf16[6,3,2048]{2,0,1:T(8,128)(2,1)S(1)} %copy.65), channel_id=1, source_target_pairs={{0,4},{4,8},{8,12},{12,16},{16,20},{20,24},{24,28},{1,5},{5,9},{9,... | collective-permute-start | bytes 221192 | tf_op jit(solution)/shard_map/ppermute | solution.py:35
  70.6 11.9 %copy-start = (f32[134,3,2048]{0,2,1:T(8,128)}, f32[134,3,2048]{0,2,1:T(8,128)S(1)}, u32[]{:S(2)}) copy-start(f32[134,3,2048]{0,2,1:T(8,128)S(1)} %maximum_convert_fusion) | copy-start | bytes 9879556
  82.5 57.6 %copy-start.28 = (s32[8]{0:T(128)S(1)}, s32[8]{0:T(128)}, u32[]{:S(2)}) copy-start(s32[8]{0:T(128)} %param.6) | copy-start | bytes 100
  82.5 83.2 %copy-start.10 = (bf16[128,2048]{1,0:T(8,128)(2,1)S(1)}, bf16[128,2048]{1,0:T(8,128)(2,1)}, u32[]{:S(2)}) copy-start(bf16[128,2048]{1,0:T(8,128)(2,1)} %param.7) | copy-start | bytes 1572868
  83.9 25.4 %collective-permute-start.4 = (bf16[128,2,2048]{0,2,1:T(8,128)(2,1)S(1)}, bf16[128,2,2048]{0,2,1:T(8,128)(2,1)S(1)}, u32[]{:S(2)}, u32[]{:S(2)}) collective-permute-start(bf16[128,2,2048]{0,2,1:T(8,128)(2,1)S(1)} %get-tuple-element.24), channel_id=1, source_target_pairs={{0,4},{4,8},{8,12},{12,16},{16,20},{20,24},{24,28},{1,5},{5,9},{9,... | collective-permute-start | bytes 3145736 | tf_op jit(solution)/shard_map/ppermute | solution.py:35
  109.3 24.6 %collective-permute-start.5 = (bf16[128,2,2048]{0,2,1:T(8,128)(2,1)S(1)}, bf16[128,2,2048]{0,2,1:T(8,128)(2,1)}, u32[]{:S(2)}, u32[]{:S(2)}) collective-permute-start(bf16[128,2,2048]{0,2,1:T(8,128)(2,1)S(1)} %collective-permute-done.4), channel_id=1, source_target_pairs={{0,4},{4,8},{8,12},{12,16},{16,20},{20,24},{24,28},{1,5},{5,9},{9,... | collective-permute-start | bytes 3145736 | tf_op jit(solution)/shard_map/ppermute | solution.py:35
  133.9 24.8 %collective-permute-start.6 = (bf16[128,2,2048]{0,2,1:T(8,128)(2,1)}, bf16[128,2,2048]{0,2,1:T(8,128)(2,1)}, u32[]{:S(2)}, u32[]{:S(2)}) collective-permute-start(bf16[128,2,2048]{0,2,1:T(8,128)(2,1)} %collective-permute-done.5), channel_id=1, source_target_pairs={{0,4},{4,8},{8,12},{12,16},{16,20},{20,24},{24,28},{1,5},{5,9},{9,... | collective-permute-start | bytes 3145736 | tf_op jit(solution)/shard_map/ppermute | solution.py:35
  158.8 24.1 %collective-permute-start.7 = (bf16[128,2,2048]{0,2,1:T(8,128)(2,1)}, bf16[128,2,2048]{0,2,1:T(8,128)(2,1)}, u32[]{:S(2)}, u32[]{:S(2)}) collective-permute-start(bf16[128,2,2048]{0,2,1:T(8,128)(2,1)} %collective-permute-done.6), channel_id=1, source_target_pairs={{0,4},{4,8},{8,12},{12,16},{16,20},{20,24},{24,28},{1,5},{5,9},{9,... | collective-permute-start | bytes 3145736 | tf_op jit(solution)/shard_map/ppermute | solution.py:35
  202.9 18.0 %copy-start.4 = (bf16[16,128,640]{2,1,0:T(8,128)(2,1)}, bf16[16,128,640]{2,1,0:T(8,128)(2,1)S(1)}, u32[]{:S(2)}) copy-start(bf16[16,128,640]{2,1,0:T(8,128)(2,1)S(1)} %fusion.2) | copy-start | bytes 7864324
  224.0 12.0 %slice-start = ((s8[5242880]{0:T(1024)(128)(4,1)}), s8[1048576]{0:T(1024)(128)(4,1)S(1)}, s32[]{:S(2)}) async-start(s8[5242880]{0:T(1024)(128)(4,1)} %bitcast.98), calls=%async_computation.2 | async-start | bytes 2097152
  236.2 46.0 %collective-permute-start.8 = (f32[128,2,2048]{0,2,1:T(8,128)S(1)}, f32[128,2,2048]{0,2,1:T(8,128)S(1)}, u32[]{:S(2)}, u32[]{:S(2)}) collective-permute-start(f32[128,2,2048]{0,2,1:T(8,128)S(1)} %fusion.26), channel_id=1, source_target_pairs={{4,0},{8,4},{12,8},{16,12},{20,16},{24,20},{28,24},{5,1},{9,5},{13... | collective-permute-start | bytes 6291464 | tf_op jit(solution)/shard_map/ppermute | solution.py:35
  282.3 45.7 %collective-permute-start.9 = (f32[128,2,2048]{0,2,1:T(8,128)S(1)}, f32[128,2,2048]{0,2,1:T(8,128)S(1)}, u32[]{:S(2)}, u32[]{:S(2)}) collective-permute-start(f32[128,2,2048]{0,2,1:T(8,128)S(1)} %fusion.29), channel_id=1, source_target_pairs={{4,0},{8,4},{12,8},{16,12},{20,16},{24,20},{28,24},{5,1},{9,5},{13... | collective-permute-start | bytes 6291464 | tf_op jit(solution)/shard_map/ppermute | solution.py:35
  328.2 47.5 %copy-start.3 = (bf16[640,1,2048]{0,2,1:T(8,128)(2,1)S(1)}, bf16[640,1,2048]{0,2,1:T(8,128)(2,1)}, u32[]{:S(2)}) copy-start(bf16[640,1,2048]{0,2,1:T(8,128)(2,1)} %copy-done.2) | copy-start | bytes 7864324
  328.3 47.5 %copy-start.5 = (bf16[16,128,640]{2,1,0:T(8,128)(2,1)S(1)}, bf16[16,128,640]{2,1,0:T(8,128)(2,1)}, u32[]{:S(2)}) copy-start(bf16[16,128,640]{2,1,0:T(8,128)(2,1)} %copy-done.4) | copy-start | bytes 7864324
  328.3 46.0 %collective-permute-start.10 = (f32[128,2,2048]{0,2,1:T(8,128)S(1)}, f32[128,2,2048]{0,2,1:T(8,128)S(1)}, u32[]{:S(2)}, u32[]{:S(2)}) collective-permute-start(f32[128,2,2048]{0,2,1:T(8,128)S(1)} %fusion.32), channel_id=1, source_target_pairs={{4,0},{8,4},{12,8},{16,12},{20,16},{24,20},{28,24},{5,1},{9,5},{13... | collective-permute-start | bytes 6291464 | tf_op jit(solution)/shard_map/ppermute | solution.py:35
  374.5 43.1 %collective-permute-start.11 = (f32[128,2,2048]{0,2,1:T(8,128)S(1)}, f32[128,2,2048]{0,2,1:T(8,128)S(1)}, u32[]{:S(2)}, u32[]{:S(2)}) collective-permute-start(f32[128,2,2048]{0,2,1:T(8,128)S(1)} %fusion.24), channel_id=1, source_target_pairs={{4,0},{8,4},{12,8},{16,12},{20,16},{24,20},{28,24},{5,1},{9,5},{13... | collective-permute-start | bytes 6291464 | tf_op jit(solution)/shard_map/ppermute | solution.py:35
  417.9 25.0 %copy-start.1 = (f32[16,128,128]{2,1,0:T(8,128)S(1)}, f32[16,128,128]{2,1,0:T(8,128)}, u32[]{:S(2)}) copy-start(f32[16,128,128]{2,1,0:T(8,128)} %fusion.53) | copy-start | bytes 3145732
  447.7 8.7 %collective-permute-start.12 = (f32[6,3,2048]{2,0,1:T(8,128)}, f32[6,3,2048]{2,0,1:T(8,128)}, u32[]{:S(2)}, u32[]{:S(2)}) collective-permute-start(f32[6,3,2048]{2,0,1:T(8,128)} %copy.79), channel_id=1, source_target_pairs={{4,0},{8,4},{12,8},{16,12},{20,16},{24,20},{28,24},{5,1},{9,5},{13... | collective-permute-start | bytes 442376 | tf_op jit(solution)/shard_map/ppermute | solution.py:35
  474.3 8.4 %copy-start.21 = (f32[3,2048]{1,0:T(4,128)S(1)}, f32[3,2048]{1,0:T(4,128)}, u32[]{:S(2)}) copy-start(f32[3,2048]{1,0:T(4,128)} %get-tuple-element.15) | copy-start | bytes 73732
  478.9 82.8 %all-to-all-start = ((bf16[128,3,2048]{2,1,0:T(4,128)(2,1)}), bf16[128,3,2048]{2,1,0:T(4,128)(2,1)S(1)}, u32[]{:S(2)}, u32[]{:S(2)}) async-start(bf16[128,3,2048]{2,1,0:T(4,128)(2,1)} %copy.81), calls=%async_computation | async-start | bytes 4194304 | tf_op jit(solution)/shard_map/all_to_all | solution.py:135
  482.6 77.3 %all-reduce.2.cloned.1.call-start = ((), (), s32[]{:S(2)}) async-start(), calls=%async_computation.1 | async-start | bytes 458752 | tf_op jit(solution)/shard_map/psum | solution.py:134
  (22 other events, 86.6 us)
Sparse Core Ops, SparseCore 0:
  487.4 72.5 all-reduce.1
